TPU v7x, 32 devices: a whole 2x2x4 slice. The times are simulated.
32 devices in a mesh: blk: 2 (over x), head: 4 (over z), weight: 4 (over y, core).
Axes of the slice: x: 2, y: 2, z: 4, core: 2. Of those that a mesh axis runs over, the one named last changes fastest.
Arguments:
- hidden_in: bfloat16 [2048, 2, 768], P(('blk', 'head', 'weight')), may hold values from -6 to 6
- qkv_weight: bfloat16 [768, 2304], replicated, may hold values from -0.21875 to 0.21875
- query_bias: float32 [768], replicated, may hold values from -3 to 3
- value_bias: float32 [768], replicated, may hold values from -0.12 to 0.12
- out_weight: bfloat16 [768, 768], replicated, may hold values from -5.75 to 5.75
- out_bias: float32 [768], replicated, may hold values from -3 to 3
- norm1_gain: float32 [768], replicated, may hold values from 0.25 to 1.75
- norm1_bias: float32 [768], replicated, may hold values from -3 to 3
- up_weight: bfloat16 [768, 3072], P(None, 'weight'), may hold values from -0.21875 to 0.21875
- up_bias: float32 [3072], P('weight'), may hold values from -3 to 3
- down_weight: bfloat16 [3072, 768], P('weight'), may hold values from -0.109375 to 0.109375
- down_bias: float32 [768], replicated, may hold values from -3 to 3
- norm2_gain: float32 [768], replicated, may hold values from 0.25 to 1.75
- norm2_bias: float32 [768], replicated, may hold values from -3 to 3
- lengths: int32 [2], replicated, may hold values from 256 to 2048, as said below
- out_cotangent: bfloat16 [2048, 2, 768], P(('blk', 'head', 'weight')), may hold values from -6 to 6
Outputs:
- layer_out: bfloat16 [2048, 2, 768], P(('blk', 'head', 'weight'))
- grad_in: float32 [2048, 2, 768], P(('blk', 'head', 'weight'))
- grad_qkv_weight: float32 [768, 2304], replicated
- grad_query_bias: float32 [768], replicated
- grad_value_bias: float32 [768], replicated
- grad_out_weight: float32 [768, 768], replicated
- grad_out_bias: float32 [768], replicated
- grad_norm1_gain: float32 [768], replicated
- grad_norm1_bias: float32 [768], replicated
- grad_up_weight: float32 [768, 3072], P(None, 'weight')
- grad_up_bias: float32 [3072], P('weight')
- grad_down_weight: float32 [3072, 768], P('weight')
- grad_down_bias: float32 [768], replicated
- grad_norm2_gain: float32 [768], replicated
- grad_norm2_bias: float32 [768], replicated
Inputs may be any that keep to these rules, and one draw needn't show every extreme that they name: Positions 0 to lengths[b] - 1 of sequence b are tokens and the rest padding; at least one sequence has no padding.
All inputs are finite; a program needn't handle non-finite values.
Results may differ from a plain program's by a relative error of at most 0.02.
Values may be sent and summed in bfloat16 or wider, within the bound.
No kernel may reach another device: no remote copies, remote signals or barrier semaphores. Data moves between devices by JAX's collectives and lax.ppermute only.
A program may use at most 128 MiB of HBM per device.

v0:
```python
import jax
import jax.numpy as jnp
from jax import lax
from jax.experimental import pallas as pl
from jax.experimental.pallas import tpu as pltpu
from jax.sharding import PartitionSpec as P


HEADS = 12
HEAD_DIM = 64
EPS = 1e-05
SQRT_HALF = 0.7071067811865476
INV_ROOT_TAU = 0.3989422804014327
SCALE = HEAD_DIM ** (-0.5)
FAR = -1e30
F32 = jnp.float32
BF16 = jnp.bfloat16
NT = (((1,), (1,)), ((), ()))
TN = (((0,), (0,)), ((), ()))


def norm_forward(resid, gain, bias):
    centre = jnp.mean(resid, axis=-1, keepdims=True)
    centred = resid - centre
    spread = jnp.mean(centred * centred, axis=-1, keepdims=True)
    rstd = lax.rsqrt(spread + EPS)
    normed = centred * rstd
    return (normed * gain + bias, normed, rstd)


def norm_backward(grad, normed, rstd, gain):
    scaled = grad * gain
    inner = (
        scaled
        - jnp.mean(scaled, axis=-1, keepdims=True)
        - normed * jnp.mean(scaled * normed, axis=-1, keepdims=True)
    )
    return (rstd * inner, jnp.sum(grad * normed, axis=0), jnp.sum(grad, axis=0))


def gelu_value(pre):
    return 0.5 * pre * (1.0 + lax.erf(pre * SQRT_HALF))


def gelu_slope(pre):
    return 0.5 * (1.0 + lax.erf(pre * SQRT_HALF)) + pre * jnp.exp(-0.5 * pre * pre) * INV_ROOT_TAU


def lane_plan(heads):
    data = heads * HEAD_DIM
    wide = -(-(data + 1 + 6 * heads) // 128) * 128
    return data, wide, data + 1, data + 1 + 3 * heads


def head_lanes(heads, head):
    data, wide, delta_at, total_at = lane_plan(heads)
    lane = lax.broadcasted_iota(jnp.int32, (1, wide), 1)

    def within(start, count):
        return (lane >= start) & (lane < start + count)

    own = within(head * HEAD_DIM, HEAD_DIM)
    extra = (
        (lane == data)
        | within(delta_at + 3 * head, 3)
        | within(total_at + 3 * head, 3)
    )
    return own.astype(F32), (own | extra).astype(BF16)


def three_parts(value):
    high = value.astype(BF16).astype(F32)
    rest = value - high
    middle = rest.astype(BF16).astype(F32)
    return high, middle, rest - middle


def spread_parts(value, start, wide):
    lane = lax.broadcasted_iota(jnp.int32, (1, wide), 1)
    out = 0.0
    for part, piece in enumerate(three_parts(value)):
        out = out + jnp.where(lane == start + part, piece, 0.0)
    return out


def on_chip(kernel, out_shape, scratch=()):
    return pl.pallas_call(
        kernel,
        out_shape=out_shape,
        scratch_shapes=list(scratch),
        compiler_params=pltpu.CompilerParams(vmem_limit_bytes=56 * 1024 * 1024),
    )


def smem():
    return pl.BlockSpec(memory_space=pltpu.SMEM)


def vmem(count):
    return [pl.BlockSpec(memory_space=pltpu.VMEM)] * count


def prepare(qkv_weight, out_weight, query_bias, value_bias, head_at, head_devs):
    heads = HEADS // head_devs
    data, wide, delta_at, total_at = lane_plan(heads)
    width = qkv_weight.shape[0]

    def kernel(at_ref, qkv_ref, out_ref, qb_ref, vb_ref, q_ref, kv_ref, bias_ref, rows_ref):
        at = at_ref[0]
        pair = at // 2
        odd = (at - 2 * pair).astype(F32)
        lane = lax.broadcasted_iota(jnp.int32, (1, wide), 1)
        keep = (lane < data).astype(F32)

        def pick(value):
            high = pltpu.roll(value, data, 1)
            return (value * (1.0 - odd) + high * odd)[:, :wide] * keep

        def columns(group):
            start = pl.multiple_of(group * width + pair * 2 * data, 128)
            return pick(qkv_ref[:, pl.ds(start, 2 * data)].astype(F32))

        q_ref[...] = (columns(0) * SCALE).astype(BF16)
        kv_ref[:, :wide] = columns(1).astype(BF16)
        kv_ref[:, wide:] = columns(2).astype(BF16)
        start = pl.ds(pl.multiple_of(pair * 2 * data, 128), 2 * data)
        ones = (lane == data).astype(F32)
        deltas = ((lane >= delta_at) & (lane < delta_at + 3 * heads)).astype(F32)
        totals = ((lane >= total_at) & (lane < total_at + 3 * heads)).astype(F32)
        query = pick(jnp.broadcast_to(qb_ref[:, start], (8, 2 * data)))[:1]
        value = pick(jnp.broadcast_to(vb_ref[:, start], (8, 2 * data)))[:1]
        bias_ref[:, :wide] = query * SCALE + ones
        bias_ref[:, wide : 2 * wide] = -totals
        bias_ref[:, 2 * wide :] = value + ones - deltas
        for hop in range(head_devs):
            source = pl.multiple_of((at ^ hop) * data, HEAD_DIM)
            rows_ref[hop * wide : hop * wide + data] = out_ref[pl.ds(source, data), :]
            rows_ref[hop * wide + data : (hop + 1) * wide] = jnp.zeros(
                (wide - data, width), BF16
            )

    return pl.pallas_call(
        kernel,
        out_shape=(
            jax.ShapeDtypeStruct((width, wide), BF16),
            jax.ShapeDtypeStruct((width, 2 * wide), BF16),
            jax.ShapeDtypeStruct((1, 3 * wide), F32),
            jax.ShapeDtypeStruct((head_devs * wide, width), BF16),
        ),
        in_specs=[smem()] + vmem(4),
        compiler_params=pltpu.CompilerParams(vmem_limit_bytes=56 * 1024 * 1024),
        name="prepare",
    )(
        head_at.reshape(1),
        qkv_weight,
        out_weight,
        query_bias.reshape(1, width),
        value_bias.reshape(1, width),
    )


def attend(query, blocks, heads, pieces):
    data, wide, _, total_at = lane_plan(heads)
    rows = query.shape[0]
    size = rows // pieces
    count = len(blocks)

    def kernel(*refs):
        query_ref, block_refs = refs[0], refs[1 : 1 + count]
        out_ref, logs_ref = refs[1 + count : 3 + count]
        piece_refs, acc_ref = refs[3 + count : -1], refs[-1]
        acc_ref[...] = jnp.zeros_like(acc_ref)

        def one_head(head):
            own, mask = head_lanes(heads, head)
            query = query_ref[...] * mask
            acc = 0.0
            for ref in block_refs:
                scores = lax.dot_general(query, ref[:, :wide], NT, preferred_element_type=F32)
                weights = jnp.exp(scores).astype(BF16)
                acc = acc + jnp.dot(weights, ref[:, wide:], preferred_element_type=F32)
            total = acc[:, data : data + 1]
            acc_ref[0] += (acc / total) * own
            acc_ref[1] += spread_parts(jnp.log(total), total_at + 3 * head, wide)

        for head in range(heads):
            one_head(head)
        out = acc_ref[0].astype(BF16)
        out_ref[...] = out
        for index, ref in enumerate(piece_refs):
            ref[...] = out[index * size : (index + 1) * size]
        logs_ref[...] = acc_ref[1].astype(BF16)

    shape = jax.ShapeDtypeStruct((rows, wide), BF16)
    small = jax.ShapeDtypeStruct((size, wide), BF16)
    return on_chip(
        kernel, (shape, shape) + (small,) * pieces, [pltpu.VMEM((2, rows, wide), F32)]
    )(query, *blocks)


def project_back(grad, out_rows, pieces):
    rows = grad.shape[0]
    wide = out_rows.shape[0] // pieces

    def kernel(grad_ref, weight_ref, *outs):
        for index, ref in enumerate(outs):
            weight = weight_ref[index * wide : (index + 1) * wide]
            ref[...] = lax.dot_general(
                grad_ref[...], weight, NT, preferred_element_type=F32
            ).astype(BF16)

    return on_chip(kernel, (jax.ShapeDtypeStruct((rows, wide), BF16),) * pieces)(grad, out_rows)


def with_stats(blocks, attended, logs, heads):
    _, wide, delta_at, _ = lane_plan(heads)
    size = blocks[0].shape[0]
    count = len(blocks)

    def kernel(*refs):
        att_ref, logs_ref, out_ref = refs[count:]
        for index, ref in enumerate(refs[:count]):
            at = slice(index * size, (index + 1) * size)
            back = ref[...].astype(F32)
            prod = back * att_ref[at].astype(F32)
            out = back + logs_ref[at].astype(F32)
            for head in range(heads):
                own, _ = head_lanes(heads, head)
                delta = jnp.sum(prod * own, axis=-1, keepdims=True)
                out = out + spread_parts(delta, delta_at + 3 * head, wide)
            out_ref[at] = out.astype(BF16)

    return on_chip(kernel, jax.ShapeDtypeStruct(attended.shape, BF16))(*blocks, attended, logs)


def total_lanes(heads):
    _, wide, _, total_at = lane_plan(heads)
    lane = lax.broadcasted_iota(jnp.int32, (1, wide), 1)
    return ((lane >= total_at) & (lane < total_at + 3 * heads)).astype(BF16)


def query_side(query, back, keyvals, heads):
    _, wide, _, _ = lane_plan(heads)
    rows = query.shape[0]

    def kernel(query_ref, back_ref, *refs):
        keyval_refs, (out_ref, acc_ref) = refs[:-2], refs[-2:]
        acc_ref[...] = jnp.zeros_like(acc_ref)

        def one_head(head, _):
            own, mask = head_lanes(heads, head)
            back_own = back_ref[...] * mask
            query_own = query_ref[...] * mask + back_own * total_lanes(heads)
            acc = 0.0
            for ref in keyval_refs:
                key = ref[:, :wide]
                scores = lax.dot_general(query_own, key, NT, preferred_element_type=F32)
                inner = lax.dot_general(back_own, ref[:, wide:], NT, preferred_element_type=F32)
                half = (jnp.exp(scores) * inner).astype(BF16)
                acc = acc + jnp.dot(half, key, preferred_element_type=F32)
            acc_ref[...] += acc * (own * SCALE)
            return 0

        lax.fori_loop(0, heads, one_head, 0)
        out_ref[...] = acc_ref[...].astype(BF16)

    return on_chip(
        kernel, jax.ShapeDtypeStruct((rows, wide), BF16), [pltpu.VMEM((rows, wide), F32)]
    )(query, back, *keyvals)


def key_side(own, queries, backs, heads):
    _, wide, _, _ = lane_plan(heads)
    rows = queries[0].shape[0]
    count = len(queries)

    def kernel(*refs):
        own_refs, refs = refs[: len(own)], refs[len(own) :]
        query_refs, back_refs = refs[:count], refs[count : 2 * count]
        out_ref, dk_ref, dv_ref = refs[2 * count :]
        keyval = jnp.concatenate([ref[...] for ref in own_refs])
        dk_ref[...] = jnp.zeros_like(dk_ref)
        dv_ref[...] = jnp.zeros_like(dv_ref)

        def one_head(head, _):
            own_lanes, mask = head_lanes(heads, head)
            key_own, value_own = keyval[:, :wide] * mask, keyval[:, wide:] * mask
            dk = dv = 0.0
            for query_ref, back_ref in zip(query_refs, back_refs):
                back_in = back_ref[...]
                query_plain = query_ref[...]
                query = query_plain + back_in * total_lanes(heads)
                scores = lax.dot_general(key_own, query, NT, preferred_element_type=F32)
                probs = jnp.exp(scores)
                inner = lax.dot_general(value_own, back_in, NT, preferred_element_type=F32)
                half = (probs * inner).astype(BF16)
                dv = dv + jnp.dot(probs.astype(BF16), back_in, preferred_element_type=F32)
                dk = dk + jnp.dot(half, query_plain, preferred_element_type=F32)
            dk_ref[...] += dk * own_lanes
            dv_ref[...] += dv * own_lanes
            return 0

        lax.fori_loop(0, heads, one_head, 0)
        out_ref[:, :wide] = dk_ref[...].astype(BF16)
        out_ref[:, wide:] = dv_ref[...].astype(BF16)

    acc = pltpu.VMEM((rows, wide), F32)
    return on_chip(
        kernel, jax.ShapeDtypeStruct((rows, 2 * wide), BF16), [acc, acc]
    )(*own, *queries, *backs)


def weight_rows(grad_query, grad_keyval, rows, attended, grad_rows, core, heads):
    data, wide, _, _ = lane_plan(heads)
    width = rows.shape[1]
    total = 4 * data

    def kernel(core_ref, dq_ref, dkv_ref, rows_ref, att_ref, grad_rows_ref, keep_ref, send_ref, sums_ref, all_ref):
        rows_in = rows_ref[...]
        for slot in range(3):
            part = dq_ref[...] if slot == 0 else dkv_ref[:, (slot - 1) * wide : slot * wide]
            out = lax.dot_general(part, rows_in, TN, preferred_element_type=F32)
            all_ref[slot * data : (slot + 1) * data] = out[:data]
            sums_ref[slot : slot + 1] = jnp.sum(part.astype(F32), axis=0, keepdims=True)
        out = lax.dot_general(
            att_ref[...], grad_rows_ref[...], TN, preferred_element_type=F32
        )
        all_ref[3 * data :] = out[:data]
        half = total // 2
        mine = pl.multiple_of(core_ref[0] * half, 64)
        theirs = pl.multiple_of((1 - core_ref[0]) * half, 64)
        keep_ref[...] = all_ref[pl.ds(mine, half), :]
        send_ref[...] = all_ref[pl.ds(theirs, half), :].astype(BF16)

    return pl.pallas_call(
        kernel,
        out_shape=(
            jax.ShapeDtypeStruct((total // 2, width), F32),
            jax.ShapeDtypeStruct((total // 2, width), BF16),
            jax.ShapeDtypeStruct((3, wide), F32),
        ),
        in_specs=[smem()] + vmem(5),
        scratch_shapes=[pltpu.VMEM((total, width), F32)],
        compiler_params=pltpu.CompilerParams(vmem_limit_bytes=56 * 1024 * 1024),
        name="weight_rows",
    )(core.reshape(1), grad_query, grad_keyval, rows, attended, grad_rows)


def input_rows(grad_query, grad_keyval, q_own, kv_own, pieces):
    width = q_own.shape[0]
    size = grad_query.shape[0] // pieces

    def kernel(dq_ref, dkv_ref, q_ref, kv_ref, *outs):
        query = (dq_ref[...].astype(F32) * (1.0 / SCALE)).astype(BF16)
        out = lax.dot_general(query, q_ref[...], NT, preferred_element_type=F32)
        out = out + lax.dot_general(
            dkv_ref[...], kv_ref[...], NT, preferred_element_type=F32
        )
        out = out.astype(BF16)
        for index, ref in enumerate(outs):
            ref[...] = out[index * size : (index + 1) * size]

    return on_chip(
        kernel, (jax.ShapeDtypeStruct((size, width), BF16),) * pieces
    )(grad_query, grad_keyval, q_own, kv_own)


def assemble(arrays, bits, orders, head_at, head_devs, heads):
    data, _, _, _ = lane_plan(heads)
    width = head_devs * data
    total = 4 * data
    size = total >> len(bits)
    step = 256 if (3 * width) % 256 == 0 else 3 * width
    steps = 3 * width // step

    def kernel(at_ref, *refs):
        ins, (qkv_ref, out_ref, all_ref, turned_ref, sems) = refs[:8], refs[8:]
        own = [at_ref[index] for index in range(len(bits))]
        head = at_ref[len(bits)]
        for number, ref in enumerate(ins):
            side, partner, last = number // 4, number // 2 % 2, number % 2
            halving = orders[side]
            doubling = halving[::-1]
            lanes = slice(side * width // 2, (side + 1) * width // 2)
            for index in range(1 << (len(doubling) - 1)):
                flip = {place: (index >> at) & 1 for at, place in enumerate(doubling[:-1])}
                flip[doubling[-1]] = last
                start = (own[0] ^ partner) * (total // 2)
                for level, place in enumerate(halving):
                    start = start + (own[place] ^ flip[place]) * (total >> (level + 2))
                group = start // data
                within = start - group * data
                for hop_at in range(head_devs):
                    row = group * width + (head ^ hop_at) * data + within
                    from_row = (index * head_devs + hop_at) * size
                    all_ref[pl.ds(pl.multiple_of(row, 8), size), lanes] = ref[
                        from_row : from_row + size
                    ].astype(F32)
        copies = [pltpu.make_async_copy(all_ref.at[pl.ds(3 * width, width)], out_ref, sems.at[0])]
        copies[0].start()
        for index in range(steps):
            at = pl.ds(index * step, step)
            turned_ref[:, at] = all_ref[at].T
            copies.append(
                pltpu.make_async_copy(
                    turned_ref.at[:, at], qkv_ref.at[:, at], sems.at[index + 1]
                )
            )
            copies[-1].start()
        for copy in copies:
            copy.wait()

    return pl.pallas_call(
        kernel,
        out_shape=(
            jax.ShapeDtypeStruct((width, 3 * width), F32),
            jax.ShapeDtypeStruct((width, width), F32),
        ),
        in_specs=[smem()] + vmem(8),
        out_specs=(pl.BlockSpec(memory_space=pl.ANY),) * 2,
        scratch_shapes=[
            pltpu.VMEM((4 * width, width), F32),
            pltpu.VMEM((width, 3 * width), F32),
            pltpu.SemaphoreType.DMA((steps + 1,)),
        ],
        compiler_params=pltpu.CompilerParams(vmem_limit_bytes=56 * 1024 * 1024),
        name="assemble",
    )(jnp.stack(bits + [head_at]).astype(jnp.int32), *arrays)


def bits_of(axis):
    return [(axis, bit) for bit in range(lax.axis_size(axis).bit_length() - 1)]


def bit_value(place):
    axis, bit = place
    return (lax.axis_index(axis) >> bit) & 1


def hop(value, axis, distance):
    return lax.ppermute(value, axis, [(i, i ^ distance) for i in range(lax.axis_size(axis))])


def trade(value, place):
    return hop(value, place[0], 1 << place[1])


def after(value, *others):
    return lax.optimization_barrier((value, *others))[0]


def spread(value):
    high = lax.reduce_precision(value, 8, 7)
    return jnp.concatenate([high, value - high]).astype(BF16)


def halve_message(value, extra, place):
    half = value.shape[0] // 2
    mine = bit_value(place)
    send = lax.dynamic_slice_in_dim(value, (1 - mine) * half, half, 0).astype(BF16)
    keep = lax.dynamic_slice_in_dim(value, mine * half, half, 0)
    return jnp.concatenate([send, spread(extra)]), keep


def halve(value, extra, place):
    message, keep = halve_message(value, extra, place)
    return settle(keep, extra, trade(message, place))


def double(value, place):
    other = trade(value, place)
    first = bit_value(place) == 0
    return jnp.concatenate([jnp.where(first, value, other), jnp.where(first, other, value)])


def settle(keep, extra, got):
    half, count = keep.shape[0], extra.shape[0]
    got = got.astype(F32)
    return (
        keep + got[:half],
        extra + got[half : half + count] + got[half + count :],
    )


def scatter_weight(value):
    for place in bits_of("weight"):
        value = value.reshape((-1, 2) + value.shape[1:])
        mine = bit_value(place)
        send = lax.dynamic_index_in_dim(value, 1 - mine, 1, keepdims=False).astype(BF16)
        keep = lax.dynamic_index_in_dim(value, mine, 1, keepdims=False)
        value = keep + trade(send, place).astype(F32)
    return value[0]


def gather_blocks(value):
    blocks = [value]
    for place in bits_of("weight")[::-1] + bits_of("blk")[1:]:
        blocks = blocks + [trade(block, place) for block in blocks]
    return blocks


def gather_head(value):
    blocks = {0: value}
    for place in bits_of("head")[::-1]:
        blocks.update(
            {at | 1 << place[1]: trade(each, place) for at, each in blocks.items()}
        )
    return [blocks[at] for at in range(len(blocks))]


def per_device(
    hidden_in,
    qkv_weight,
    query_bias,
    value_bias,
    out_weight,
    out_bias,
    norm1_gain,
    norm1_bias,
    up_weight,
    up_bias,
    down_weight,
    down_bias,
    norm2_gain,
    norm2_bias,
    lengths,
    out_cotangent,
):
    rows_here, _, width = hidden_in.shape
    head_devs = lax.axis_size("head")
    weight_devs = lax.axis_size("weight")
    blk = lax.axis_index("blk")
    head_at = lax.axis_index("head")
    weight_at = lax.axis_index("weight")
    first_seq = (blk & 1) == 0
    heads = HEADS // head_devs
    data, wide, _, _ = lane_plan(heads)
    tokens = 2 * rows_here
    swap = ("blk", 0)

    def to_sequence(value):
        zero, one = value[:, 0], value[:, 1]
        mine = jnp.where(first_seq, zero, one)
        other = trade(jnp.where(first_seq, one, zero), swap)
        return jnp.concatenate([mine, other], axis=0)

    def from_sequence(value, narrow):
        mine = value[:rows_here]
        other = trade(value[rows_here:].astype(narrow), swap).astype(value.dtype)
        return jnp.stack(
            [jnp.where(first_seq, mine, other), jnp.where(first_seq, other, mine)], axis=1
        )

    flat = to_sequence(hidden_in)
    q_own, kv_own, bias_own, out_rows = prepare(
        after(qkv_weight, flat), out_weight, query_bias, value_bias, head_at, head_devs
    )
    hops = gather_head(flat)
    split = head_devs // 2
    near, far = jnp.concatenate(hops[:split]), jnp.concatenate(hops[split:])
    cotangent = to_sequence(after(out_cotangent, flat)).astype(F32)

    def project(part, first):
        index = jnp.arange(part.shape[0], dtype=jnp.int32)
        source = head_at ^ (first + index // tokens)
        within = index % tokens
        source_blk = blk ^ (within // rows_here)
        position = (
            (source_blk * head_devs + source) * weight_devs + weight_at
        ) * rows_here + within % rows_here
        valid = position < jnp.where(first_seq, lengths[0], lengths[1])
        lane = jnp.arange(2 * wide, dtype=jnp.int32)
        masked = jnp.where((lane == data)[None, :] & ~valid[:, None], FAR, 0.0)
        return (
            jnp.dot(part, kv_own, preferred_element_type=F32) + bias_own[:, wide:] + masked
        ).astype(BF16)

    own_keyvals = [project(near, 0), project(far, split)]
    keyvals = gather_blocks(own_keyvals[0])
    keyvals = keyvals + gather_blocks(own_keyvals[1])
    rows = jnp.concatenate([near, far])
    query = (
        jnp.dot(rows, q_own, preferred_element_type=F32) + bias_own[:, :wide]
    ).astype(BF16)
    attended, logs, *parts = attend(query, keyvals, heads, head_devs)
    queries = gather_blocks(after(query, attended))
    returned = [parts[0]] + [hop(parts[at], "head", at) for at in range(1, head_devs)]
    returned = jnp.concatenate(returned, axis=1)
    resid1 = flat.astype(F32) + jnp.dot(returned, out_rows, preferred_element_type=F32) + out_bias
    hidden1, normed1, rstd1 = norm_forward(resid1, norm1_gain, norm1_bias)
    gathered = lax.all_gather(hidden1.astype(BF16), "weight", axis=0, tiled=True)
    pre = jnp.dot(gathered, up_weight, preferred_element_type=F32) + up_bias
    active = gelu_value(pre).astype(BF16)
    mixed = scatter_weight(
        jnp.dot(active, down_weight, preferred_element_type=F32).reshape(
            weight_devs, tokens, width
        )
    )
    resid2 = hidden1 + mixed + down_bias
    final, normed2, rstd2 = norm_forward(resid2, norm2_gain, norm2_bias)
    grad_resid2, grad_norm2_gain, grad_norm2_bias = norm_backward(
        cotangent, normed2, rstd2, norm2_gain
    )
    grad_down_bias = jnp.sum(grad_resid2, axis=0)
    mixed_all = lax.all_gather(grad_resid2.astype(BF16), "weight", axis=0, tiled=True)
    grad_pre = lax.dot_general(
        mixed_all, down_weight, NT, preferred_element_type=F32
    ) * gelu_slope(pre)
    grad_up_bias = jnp.sum(grad_pre, axis=0)
    grad_pre_half = grad_pre.astype(BF16)
    back_hidden = scatter_weight(
        lax.dot_general(grad_pre_half, up_weight, NT, preferred_element_type=F32).reshape(
            weight_devs, tokens, width
        )
    )
    grad_down_weight = lax.dot_general(active, mixed_all, TN, preferred_element_type=F32)
    grad_up_weight = lax.dot_general(gathered, grad_pre_half, TN, preferred_element_type=F32)
    up_extra = jnp.pad(grad_up_bias[None], ((0, 7), (0, 0)))
    ffn_keep = jnp.where(first_seq, grad_up_weight, grad_down_weight)
    ffn_send = jnp.concatenate(
        [
            jnp.where(first_seq, grad_down_weight, grad_up_weight).astype(BF16),
            spread(up_extra),
        ]
    )
    grad_hidden1 = grad_resid2 + back_hidden
    grad_resid1, grad_norm1_gain, grad_norm1_bias = norm_backward(
        grad_hidden1, normed1, rstd1, norm1_gain
    )
    grad_out_bias = jnp.sum(grad_resid1, axis=0)
    grad_half, ffn_keep, ffn_send = lax.optimization_barrier(
        (grad_resid1.astype(BF16), ffn_keep, ffn_send)
    )
    ffn_got = trade(ffn_send, swap)
    ffn_places = bits_of("blk")[1:] + bits_of("head")
    layer_out = from_sequence(after(final.astype(BF16), grad_half), BF16)
    backs = project_back(grad_half, out_rows, head_devs)
    backs = [backs[0]] + [hop(backs[at], "head", at) for at in range(1, head_devs)]
    back = with_stats(backs, attended, logs, heads)
    back_blocks = gather_blocks(back)
    grad_late = after(grad_half, back)
    grad_rows = jnp.concatenate(
        [grad_late] + [hop(grad_late, "head", at) for at in range(1, head_devs)]
    )
    grad_query = query_side(query, back, keyvals, heads)
    ffn, up_extra = settle(ffn_keep, up_extra, after(ffn_got, grad_query))
    ffn_message, ffn_keep = halve_message(ffn, up_extra, ffn_places[0])
    ffn_got = trade(ffn_message, ffn_places[0])
    grad_keyval = key_side(own_keyvals, queries, back_blocks, heads)
    ffn, up_extra = settle(ffn_keep, up_extra, after(ffn_got, grad_keyval))
    for place in ffn_places[1:]:
        ffn, up_extra = halve(ffn, up_extra, place)
    ffn = ffn.astype(BF16)

    weight_bits, blk_bits = bits_of("weight"), bits_of("blk")
    core, middle, outer = weight_bits[0], weight_bits[1:], blk_bits
    keep, send, column_sums = weight_rows(
        grad_query, grad_keyval, rows, attended, grad_rows, bit_value(core), heads
    )
    column_sums = column_sums[:, :data]
    bias_rows = lax.dynamic_update_slice(
        jnp.zeros((2, head_devs, data), F32),
        jnp.stack([column_sums[0], column_sums[2]])[:, None],
        (0, head_at, 0),
    ).reshape(2, width)
    extra = jnp.concatenate(
        [
            bias_rows,
            jnp.stack([
                grad_out_bias,
                grad_norm1_gain,
                grad_norm1_bias,
                grad_norm2_gain,
                grad_norm2_bias,
                grad_down_bias,
            ]),
        ]
    )
    count = extra.shape[0]
    got = trade(jnp.concatenate([send, spread(extra)]), core)
    value, extra = settle(keep, extra, got)
    lane_half = width // 2
    orders = (middle + outer, outer + middle)
    sides = [
        (value[:, at * lane_half : (at + 1) * lane_half], extra[:, at * lane_half : (at + 1) * lane_half])
        for at in range(2)
    ]
    for level in range(len(middle + outer)):
        out = [halve_message(*sides[at], orders[at][level]) for at in range(2)]
        messages = lax.optimization_barrier((out[0][0], out[1][0]))
        got = [trade(messages[at], orders[at][level]) for at in range(2)]
        sides = [settle(out[at][1], sides[at][1], got[at]) for at in range(2)]
    sides = [jnp.concatenate([part.astype(BF16), spread(small)]) for part, small in sides]
    piece = jnp.concatenate(sides, axis=1)
    partial = input_rows(grad_query, grad_keyval, q_own, kv_own, head_devs)
    piece, *partial = lax.optimization_barrier((piece, *partial))
    pieces = gather_head(piece)
    size = piece.shape[0] - 2 * count
    small = sum(
        each[size : size + count].astype(F32) + each[size + count :].astype(F32)
        for each in pieces
    )
    stacked = jnp.concatenate([each[:size] for each in pieces])
    for place in ffn_places[:0:-1]:
        ffn = double(ffn, place)
    left, right = ffn[:, :lane_half], ffn[:, lane_half:]
    first_row = bit_value(ffn_places[0]) == 0

    def in_order(first, mine, other):
        return jnp.where(first, mine, other), jnp.where(first, other, mine)

    left_got, right_got = trade(left, ffn_places[0]), trade(right, swap)
    left = jnp.concatenate(in_order(first_row, left, left_got))
    right = jnp.concatenate(in_order(first_seq, right, right_got))
    left_got, right_got = trade(left, swap), trade(right, ffn_places[0])
    half_rows = right.shape[0] // 2
    up_left, down_left = in_order(first_seq, left, left_got)
    up_right = jnp.concatenate(in_order(first_row, right[:half_rows], right_got[:half_rows]))
    down_right = jnp.concatenate(in_order(first_row, right[half_rows:], right_got[half_rows:]))
    sides = [stacked[:, :lane_half], stacked[:, lane_half:]]
    count = len(middle + outer)
    for level in range(count - 1):
        got = [trade(sides[at], orders[at][::-1][level]) for at in range(2)]
        sides = [jnp.concatenate([sides[at], got[at]]) for at in range(2)]
    last = [trade(sides[at], orders[at][0]) for at in range(2)]
    arrays = [
        each
        for at in range(2)
        for each in (sides[at], last[at], trade(sides[at], core), trade(last[at], core))
    ]
    slot = {place: at for at, place in enumerate([core] + middle + outer)}
    grad_qkv_weight, grad_out_weight = assemble(
        arrays,
        [bit_value(place) for place in [core] + middle + outer],
        [[slot[at] for at in order] for order in orders],
        head_at,
        head_devs,
        heads,
    )

    partial = lax.optimization_barrier((*partial, stacked))[:-1]
    grad_in = grad_resid1 + partial[0].astype(F32)
    for at in range(1, head_devs):
        part = hop(partial[at], "head", at)
        grad_in = grad_in + part.astype(F32)
    grad_in = from_sequence(grad_in, BF16)
    return (
        layer_out,
        grad_in,
        grad_qkv_weight,
        small[0],
        small[1],
        grad_out_weight,
        small[2],
        small[3],
        small[4],
        jnp.concatenate([up_left, up_right], axis=1).astype(F32),
        up_extra[0],
        jnp.concatenate([down_left, down_right], axis=1).astype(F32),
        small[7],
        small[5],
        small[6],
    )


def solution(mesh):
    placed = (
        P(("blk", "head", "weight"), None, None),
        P(),
        P(),
        P(),
        P(),
        P(),
        P(),
        P(),
        P(None, "weight"),
        P("weight"),
        P("weight", None),
        P(),
        P(),
        P(),
        P(),
        P(("blk", "head", "weight"), None, None),
    )

    return jax.shard_map(
        per_device,
        mesh=mesh,
        in_specs=placed,
        out_specs=(
            P(("blk", "head", "weight"), None, None),
            P(("blk", "head", "weight"), None, None),
            P(),
            P(),
            P(),
            P(),
            P(),
            P(),
            P(),
            P(None, "weight"),
            P("weight"),
            P("weight", None),
            P(),
            P(),
            P(),
        ),
        check_vma=False,
    )
```

profile of v0, /device:TPU:0, one launch (start us, length us, event | category | flops | bytes accessed | tf_op | source)
XLA Modules:
  0.0 325.2 jit_solution(18404190784059524075)
XLA Ops:
  12.7 4.8 %prepare.1 = (bf16[768,256]{1,0:T(8,128)(2,1)}, bf16[768,512]{1,0:T(8,128)(2,1)}, f32[1,768]{1,0:T(1,128)}, bf16[1024,768]{1,0:T(8,128)(2,1)}) custom-call(s32[1]{0:T(128)} %bitcast.2.at_ref, bf16[768,2304]{1,0:T(8,128)(2,1)} %qkv_ref, bf16[768,768]{1,0:T(8,128)(2,1)} %out_ref.1, f32[1,768]{1,0:T(1,128)} %reshape.190.qb_ref, f32[1,768]{1,0:T(1,128)} %reshape.191.vb_ref), custom_call_target="tpu_custom_call" | custom-call | tf_op jit(solution)/shard_map/prepare/pallas_call | solution.py:142
  31.4 4.4 %collective-permute-done.7.refs_6_.refs_5_ = bf16[256,512]{1,0:T(8,128)(2,1)S(1)} collective-permute-done((bf16[256,512]{1,0:T(8,128)(2,1)S(1)}, bf16[256,512]{1,0:T(8,128)(2,1)S(1)}, u32[]{:S(2)}, u32[]{:S(2)}) %collective-permute-start.7) | collective-permute-done | bytes 262176 | tf_op jit(solution)/shard_map/ppermute | solution.py:441
  39.5 6.3 %shard_map.271 = (bf16[512,256]{1,0:T(8,128)(2,1)}, bf16[512,256]{1,0:T(8,128)(2,1)}, bf16[128,256]{1,0:T(8,128)(2,1)}, bf16[128,256]{1,0:T(8,128)(2,1)}, bf16[1...) custom-call(bf16[512,256]{1,0:T(8,128)(2,1)} %fusion.9.refs_0_.query_ref.refs_2_, bf16[256,512]{1,0:T(8,128)(2,1)} %copy-done.5, ...), custom_call_target="tpu_custom_call" | custom-call | tf_op jit(solution)/shard_map/pallas_call | solution.py:196
  52.2 4.0 %collective-permute-done.12 = bf16[128,256]{1,0:T(8,128)(2,1)S(1)} collective-permute-done((bf16[128,256]{1,0:T(8,128)(2,1)}, bf16[128,256]{1,0:T(8,128)(2,1)S(1)}, u32[]{:S(2)}, u32[]{:S(2)}) %collective-permute-start.12) | collective-permute-done | bytes 65568 | tf_op jit(solution)/shard_map/ppermute | solution.py:441
  58.0 8.6 %all_gather.6 = bf16[512,768]{1,0:T(8,128)(2,1)S(1)} all-gather(bf16[128,768]{1,0:T(8,128)(2,1)S(1)} %fusion.33), channel_id=1, replica_groups=mesh['blk'=2,'head'=4,'weight'=4] {'weight'}, dimensions={0}, use_global_device_ids=true | all-gather | bytes 983040 | tf_op jit(solution)/shard_map/all_gather | solution.py:591
  77.1 5.8 %collective-permute-done.14 = bf16[1,128,768]{2,1,0:T(8,128)(2,1)S(1)} collective-permute-done((bf16[1,128,768]{2,1,0:T(8,128)(2,1)S(1)}, bf16[1,128,768]{2,1,0:T(8,128)(2,1)S(1)}, u32[]{:S(2)}, u32[]{:S(2)}) %collective-permute-start.14) | collective-permute-done | bytes 196640 | tf_op jit(solution)/shard_map/ppermute | solution.py:441
  84.0 8.1 %all_gather.7 = bf16[512,768]{1,0:T(8,128)(2,1)S(1)} all-gather(bf16[128,768]{1,0:T(8,128)(2,1)S(1)} %convert_element_type.192), channel_id=1, replica_groups=mesh['blk'=2,'head'=4,'weight'=4] {'weight'}, dimensions={0}, use_global_device_ids=true | all-gather | bytes 983040 | tf_op jit(solution)/shard_map/all_gather | solution.py:605
  100.3 5.7 %collective-permute-done.17 = bf16[1,128,768]{2,1,0:T(8,128)(2,1)S(1)} collective-permute-done((bf16[1,128,768]{2,1,0:T(8,128)(2,1)S(1)}, bf16[1,128,768]{2,1,0:T(8,128)(2,1)S(1)}, u32[]{:S(2)}, u32[]{:S(2)}) %collective-permute-start.17) | collective-permute-done | bytes 196640 | tf_op jit(solution)/shard_map/ppermute | solution.py:441
  115.6 4.2 %collective-permute-done.20.refs_2_ = bf16[128,256]{1,0:T(8,128)(2,1)S(1)} collective-permute-done((bf16[128,256]{1,0:T(8,128)(2,1)}, bf16[128,256]{1,0:T(8,128)(2,1)S(1)}, u32[]{:S(2)}, u32[]{:S(2)}) %collective-permute-start.20) | collective-permute-done | bytes 65568 | tf_op jit(solution)/shard_map/ppermute | solution.py:441
  128.0 5.2 %collective-permute-done.30 = bf16[128,768]{1,0:T(8,128)(2,1)S(1)} collective-permute-done((bf16[128,768]{1,0:T(8,128)(2,1)S(1)}, bf16[128,768]{1,0:T(8,128)(2,1)S(1)}, u32[]{:S(2)}, u32[]{:S(2)}) %collective-permute-start.30) | collective-permute-done | bytes 196640 | tf_op jit(solution)/shard_map/ppermute | solution.py:441
  133.2 9.3 %collective-permute-done.29 = bf16[128,768]{1,0:T(8,128)(2,1)S(1)} collective-permute-done((bf16[128,768]{1,0:T(8,128)(2,1)S(1)}, bf16[128,768]{1,0:T(8,128)(2,1)S(1)}, u32[]{:S(2)}, u32[]{:S(2)}) %collective-permute-start.29) | collective-permute-done | bytes 196640 | tf_op jit(solution)/shard_map/ppermute | solution.py:441
  143.3 8.8 %shard_map.274.dq_ref = bf16[512,256]{1,0:T(8,128)(2,1)} custom-call(bf16[512,256]{1,0:T(8,128)(2,1)} %fusion.9.refs_0_.query_ref.refs_2_, bf16[512,256]{1,0:T(8,128)(2,1)} %shard_map.273.back_ref.refs_6_, bf16[256,512]{1,0:T(8,128)(2,1)} %copy-done.5, bf16[256,512]{1,0:T(8,128)(2,1)} %copy-done.11, bf16[256,512]{1,0:T(8,128)(2,1)} %copy-done.13, ...), custom_call_target="tpu_custom_call" | custom-call | tf_op jit(solution)/shard_map/pallas_call | solution.py:267
  154.6 9.8 %shard_map.275.dkv_ref = bf16[512,512]{1,0:T(8,128)(2,1)} custom-call(bf16[256,512]{1,0:T(8,128)(2,1)} %copy-done.5, bf16[256,512]{1,0:T(8,128)(2,1)} %copy-done.6, bf16[512,256]{1,0:T(8,128)(2,1)} %fusion.9.refs_0_.query_ref.refs_2_, bf16[512,256]{1,0:T(8,128)(2,1)} %copy-done.27, bf16[512,256]{1,0:T(8,128)(2,1)} %copy-done.29, ...), custom_call_target="tpu_custom_call" | custom-call | tf_op jit(solution)/shard_map/pallas_call | solution.py:308
  180.1 24.1 %collective-permute-done.51 = bf16[784,768]{1,0:T(8,128)(2,1)S(1)} collective-permute-done((bf16[784,768]{1,0:T(8,128)(2,1)S(1)}, bf16[784,768]{1,0:T(8,128)(2,1)S(1)}, u32[]{:S(2)}, u32[]{:S(2)}) %collective-permute-start.51) | collective-permute-done | bytes 1204256 | tf_op jit(solution)/shard_map/ppermute | solution.py:441
  214.6 5.3 %collective-permute-done.37 = bf16[112,768]{1,0:T(8,128)(2,1)S(1)} collective-permute-done((bf16[112,768]{1,0:T(8,128)(2,1)S(1)}, bf16[112,768]{1,0:T(8,128)(2,1)S(1)}, u32[]{:S(2)}, u32[]{:S(2)}) %collective-permute-start.37) | collective-permute-done | bytes 172064 | tf_op jit(solution)/shard_map/ppermute | solution.py:441
  220.8 14.4 %collective-permute-done.36 = bf16[112,768]{1,0:T(8,128)(2,1)S(1)} collective-permute-done((bf16[112,768]{1,0:T(8,128)(2,1)S(1)}, bf16[112,768]{1,0:T(8,128)(2,1)S(1)}, u32[]{:S(2)}, u32[]{:S(2)}) %collective-permute-start.36) | collective-permute-done | bytes 172064 | tf_op jit(solution)/shard_map/ppermute | solution.py:441
  244.4 25.4 %collective-permute-done.53 = bf16[208,768]{1,0:T(8,128)(2,1)S(1)} collective-permute-done((bf16[208,768]{1,0:T(8,128)(2,1)S(1)}, bf16[208,768]{1,0:T(8,128)(2,1)S(1)}, u32[]{:S(2)}, u32[]{:S(2)}) %collective-permute-start.53) | collective-permute-done | bytes 319520 | tf_op jit(solution)/shard_map/ppermute | solution.py:441
  272.3 5.7 %collective-permute-done.43 = bf16[384,384]{1,0:T(8,128)(2,1)S(1)} collective-permute-done((bf16[384,384]{1,0:T(8,128)(2,1)S(1)}, bf16[384,384]{1,0:T(8,128)(2,1)S(1)}, u32[]{:S(2)}, u32[]{:S(2)}) %collective-permute-start.43) | collective-permute-done | bytes 294944 | tf_op jit(solution)/shard_map/ppermute | solution.py:441
  280.2 5.5 %collective-permute-done.54 = bf16[192,768]{1,0:T(8,128)(2,1)S(1)} collective-permute-done((bf16[192,768]{1,0:T(8,128)(2,1)S(1)}, bf16[192,768]{1,0:T(8,128)(2,1)S(1)}, u32[]{:S(2)}, u32[]{:S(2)}) %collective-permute-start.54) | collective-permute-done | bytes 294944 | tf_op jit(solution)/shard_map/ppermute | solution.py:441
  287.3 6.7 %collective-permute-done.44.refs_1_ = bf16[768,384]{1,0:T(8,128)(2,1)S(1)} collective-permute-done((bf16[768,384]{1,0:T(8,128)(2,1)S(1)}, bf16[768,384]{1,0:T(8,128)(2,1)S(1)}, u32[]{:S(2)}, u32[]{:S(2)}) %collective-permute-start.44) | collective-permute-done | bytes 589856 | tf_op jit(solution)/shard_map/ppermute | solution.py:441
  295.7 6.1 %collective-permute-done.48.refs_5_ = bf16[768,384]{1,0:T(8,128)(2,1)S(1)} collective-permute-done((bf16[768,384]{1,0:T(8,128)(2,1)S(1)}, bf16[768,384]{1,0:T(8,128)(2,1)S(1)}, u32[]{:S(2)}, u32[]{:S(2)}) %collective-permute-start.48) | collective-permute-done | bytes 589856 | tf_op jit(solution)/shard_map/ppermute | solution.py:441
  302.5 4.7 %collective-permute-done.57 = bf16[384,384]{1,0:T(8,128)(2,1)S(1)} collective-permute-done((bf16[384,384]{1,0:T(8,128)(2,1)S(1)}, bf16[384,384]{1,0:T(8,128)(2,1)S(1)}, u32[]{:S(2)}, u32[]{:S(2)}) %collective-permute-start.57) | collective-permute-done | bytes 294944 | tf_op jit(solution)/shard_map/ppermute | solution.py:441
  310.3 6.6 %assemble.1 = (f32[768,2304]{1,0:T(8,128)}, f32[768,768]{1,0:T(8,128)}) custom-call(s32[4]{0:T(128)} %pad_add_fusion.1.at_ref, bf16[768,384]{1,0:T(8,128)(2,1)} %copy-done.3, bf16[768,384]{1,0:T(8,128)(2,1)} %copy-done.20, bf16[768,384]{1,0:T(8,128)(2,1)} %copy-done.19, bf16[768,384]{1,0:T(8,128)(2,1)} %copy-done.23, bf16[768,384]{1,0:T(8,128)(2,1)} %copy-done.4, ...), custom_call_target="tpu_custom_call" | custom-call | tf_op jit(solution)/shard_map/assemble/pallas_call | solution.py:413
  316.9 4.7 %collective-permute-done.56 = bf16[768,384]{1,0:T(8,128)(2,1)S(1)} collective-permute-done((bf16[768,384]{1,0:T(8,128)(2,1)S(1)}, bf16[768,384]{1,0:T(8,128)(2,1)S(1)}, u32[]{:S(2)}, u32[]{:S(2)}) %collective-permute-start.56) | collective-permute-done | bytes 589856 | tf_op jit(solution)/shard_map/ppermute | solution.py:441
  (361 shorter events, 127.7 us)
Async XLA Ops:
  122.8 19.7 %collective-permute-start.25 = (bf16[512,256]{1,0:T(8,128)(2,1)}, bf16[512,256]{1,0:T(8,128)(2,1)S(1)}, u32[]{:S(2)}, u32[]{:S(2)}) collective-permute-start(bf16[512,256]{1,0:T(8,128)(2,1)} %shard_map.273.back_ref.refs_6_), channel_id=1, source_target_pairs={{0,2},{1,3},{2,0},{3,1},{4,6},{5,7},{6,4},{7,5},{8,10},{9,11},{10,... | collective-permute-start | bytes 786440 | tf_op jit(solution)/shard_map/ppermute | solution.py:441
  125.9 16.6 %collective-permute-start.29 = (bf16[128,768]{1,0:T(8,128)(2,1)S(1)}, bf16[128,768]{1,0:T(8,128)(2,1)S(1)}, u32[]{:S(2)}, u32[]{:S(2)}) collective-permute-start(bf16[128,768]{1,0:T(8,128)(2,1)S(1)} %copy-done.8), channel_id=1, source_target_pairs={{0,8},{4,12},{8,0},{12,4},{1,9},{5,13},{9,1},{13,5},{2,10},{6,14},... | collective-permute-start | bytes 589832 | tf_op jit(solution)/shard_map/ppermute | solution.py:441
  126.3 25.8 %collective-permute-start.28 = (bf16[128,768]{1,0:T(8,128)(2,1)S(1)}, bf16[128,768]{1,0:T(8,128)(2,1)}, u32[]{:S(2)}, u32[]{:S(2)}) collective-permute-start(bf16[128,768]{1,0:T(8,128)(2,1)S(1)} %copy-done.8), channel_id=1, source_target_pairs={{0,4},{4,0},{8,12},{12,8},{1,5},{5,1},{9,13},{13,9},{2,6},{6,2},{1... | collective-permute-start | bytes 589832 | tf_op jit(solution)/shard_map/ppermute | solution.py:441
  128.0 26.0 %collective-permute-start.23 = (bf16[512,256]{1,0:T(8,128)(2,1)S(1)}, bf16[512,256]{1,0:T(8,128)(2,1)S(1)}, u32[]{:S(2)}, u32[]{:S(2)}) collective-permute-start(bf16[512,256]{1,0:T(8,128)(2,1)S(1)} %copy-done.7), channel_id=1, source_target_pairs={{0,1},{1,0},{2,3},{3,2},{4,5},{5,4},{6,7},{7,6},{8,9},{9,8},{10,11... | collective-permute-start | bytes 786440 | tf_op jit(solution)/shard_map/ppermute | solution.py:441
  133.2 20.8 %collective-permute-start.24 = (bf16[512,256]{1,0:T(8,128)(2,1)S(1)}, bf16[512,256]{1,0:T(8,128)(2,1)}, u32[]{:S(2)}, u32[]{:S(2)}) collective-permute-start(bf16[512,256]{1,0:T(8,128)(2,1)S(1)} %collective-permute-done.22.refs_3_), channel_id=1, source_target_pairs={{0,1},{1,0},{2,3},{3,2},{4,5},{5,4},{6,7},{7,6},{8,9},{9,8},{10,11... | collective-permute-start | bytes 786440 | tf_op jit(solution)/shard_map/ppermute | solution.py:441
  172.6 47.2 %collective-permute-start.18 = (bf16[64,768]{1,0:T(8,128)(2,1)S(1)}, bf16[64,768]{1,0:T(8,128)(2,1)S(1)}, u32[]{:S(2)}, u32[]{:S(2)}) collective-permute-start(bf16[64,768]{1,0:T(8,128)(2,1)S(1)} %slice.223), channel_id=1, source_target_pairs={{0,16},{16,0},{1,17},{17,1},{2,18},{18,2},{3,19},{19,3},{4,20},{20... | collective-permute-start | bytes 294920 | tf_op jit(solution)/shard_map/ppermute | solution.py:441
  173.2 31.0 %collective-permute-start.51 = (bf16[784,768]{1,0:T(8,128)(2,1)S(1)}, bf16[784,768]{1,0:T(8,128)(2,1)S(1)}, u32[]{:S(2)}, u32[]{:S(2)}) collective-permute-start(bf16[784,768]{1,0:T(8,128)(2,1)S(1)} %pad_maximum_fusion), channel_id=1, source_target_pairs={{0,16},{16,0},{1,17},{17,1},{2,18},{18,2},{3,19},{19,3},{4,20},{20... | collective-permute-start | bytes 3612680 | tf_op jit(solution)/shard_map/ppermute | solution.py:441
  178.3 26.4 %collective-permute-start.32 = (bf16[208,384]{1,0:T(8,128)(2,1)S(1)}, bf16[208,384]{1,0:T(8,128)(2,1)S(1)}, u32[]{:S(2)}, u32[]{:S(2)}) collective-permute-start(bf16[208,384]{1,0:T(8,128)(2,1)S(1)} %pad_maximum_fusion.15), channel_id=1, source_target_pairs={{0,2},{1,3},{2,0},{3,1},{4,6},{5,7},{6,4},{7,5},{8,10},{9,11},{10,... | collective-permute-start | bytes 479240 | tf_op jit(solution)/shard_map/ppermute | solution.py:441
  179.6 27.1 %collective-permute-start.33 = (bf16[208,384]{1,0:T(8,128)(2,1)S(1)}, bf16[208,384]{1,0:T(8,128)(2,1)S(1)}, u32[]{:S(2)}, u32[]{:S(2)}) collective-permute-start(bf16[208,384]{1,0:T(8,128)(2,1)S(1)} %pad_maximum_fusion.16), channel_id=1, source_target_pairs={{0,16},{16,0},{1,17},{17,1},{2,18},{18,2},{3,19},{19,3},{4,20},{20... | collective-permute-start | bytes 479240 | tf_op jit(solution)/shard_map/ppermute | solution.py:441
  212.3 31.0 %collective-permute-start.52 = (bf16[400,768]{1,0:T(8,128)(2,1)S(1)}, bf16[400,768]{1,0:T(8,128)(2,1)S(1)}, u32[]{:S(2)}, u32[]{:S(2)}) collective-permute-start(bf16[400,768]{1,0:T(8,128)(2,1)S(1)} %pad_maximum_fusion.3), channel_id=1, source_target_pairs={{0,4},{4,0},{8,12},{12,8},{1,5},{5,1},{9,13},{13,9},{2,6},{6,2},{1... | collective-permute-start | bytes 1843208 | tf_op jit(solution)/shard_map/ppermute | solution.py:441
  214.5 20.7 %collective-permute-start.36 = (bf16[112,768]{1,0:T(8,128)(2,1)S(1)}, bf16[112,768]{1,0:T(8,128)(2,1)S(1)}, u32[]{:S(2)}, u32[]{:S(2)}) collective-permute-start(bf16[112,768]{1,0:T(8,128)(2,1)S(1)} %maximum_maximum_fusion), channel_id=1, source_target_pairs={{0,4},{4,0},{8,12},{12,8},{1,5},{5,1},{9,13},{13,9},{2,6},{6,2},{1... | collective-permute-start | bytes 516104 | tf_op jit(solution)/shard_map/ppermute | solution.py:441
  219.8 17.3 %collective-permute-start.38 = (bf16[112,768]{1,0:T(8,128)(2,1)S(1)}, bf16[112,768]{1,0:T(8,128)(2,1)S(1)}, u32[]{:S(2)}, u32[]{:S(2)}) collective-permute-start(bf16[112,768]{1,0:T(8,128)(2,1)S(1)} %collective-permute-done.37), channel_id=1, source_target_pairs={{0,4},{4,0},{8,12},{12,8},{1,5},{5,1},{9,13},{13,9},{2,6},{6,2},{1... | collective-permute-start | bytes 516104 | tf_op jit(solution)/shard_map/ppermute | solution.py:441
  237.2 34.6 %collective-permute-start.39 = (bf16[128,768]{1,0:T(8,128)(2,1)S(1)}, bf16[128,768]{1,0:T(8,128)(2,1)S(1)}, u32[]{:S(2)}, u32[]{:S(2)}) collective-permute-start(bf16[128,768]{1,0:T(8,128)(2,1)S(1)} %copy-done.52), channel_id=1, source_target_pairs={{0,4},{4,0},{8,12},{12,8},{1,5},{5,1},{9,13},{13,9},{2,6},{6,2},{1... | collective-permute-start | bytes 589832 | tf_op jit(solution)/shard_map/ppermute | solution.py:441
  237.3 34.6 %collective-permute-start.40 = (bf16[128,768]{1,0:T(8,128)(2,1)S(1)}, bf16[128,768]{1,0:T(8,128)(2,1)S(1)}, u32[]{:S(2)}, u32[]{:S(2)}) collective-permute-start(bf16[128,768]{1,0:T(8,128)(2,1)S(1)} %copy-done.51), channel_id=1, source_target_pairs={{0,8},{4,12},{8,0},{12,4},{1,9},{5,13},{9,1},{13,5},{2,10},{6,14},... | collective-permute-start | bytes 589832 | tf_op jit(solution)/shard_map/ppermute | solution.py:441
  240.0 31.8 %collective-permute-start.41 = (bf16[128,768]{1,0:T(8,128)(2,1)S(1)}, bf16[128,768]{1,0:T(8,128)(2,1)S(1)}, u32[]{:S(2)}, u32[]{:S(2)}) collective-permute-start(bf16[128,768]{1,0:T(8,128)(2,1)S(1)} %copy-done.50), channel_id=1, source_target_pairs={{0,12},{4,8},{8,4},{12,0},{1,13},{5,9},{9,5},{13,1},{2,14},{6,10},... | collective-permute-start | bytes 589832 | tf_op jit(solution)/shard_map/ppermute | solution.py:441
  241.7 38.1 %collective-permute-start.47 = (bf16[384,384]{1,0:T(8,128)(2,1)S(1)}, bf16[384,384]{1,0:T(8,128)(2,1)S(1)}, u32[]{:S(2)}, u32[]{:S(2)}) collective-permute-start(bf16[384,384]{1,0:T(8,128)(2,1)S(1)} %get-tuple-element.188), channel_id=1, source_target_pairs={{0,2},{1,3},{2,0},{3,1},{4,6},{5,7},{6,4},{7,5},{8,10},{9,11},{10,... | collective-permute-start | bytes 884744 | tf_op jit(solution)/shard_map/ppermute | solution.py:441
  243.6 26.2 %collective-permute-start.53 = (bf16[208,768]{1,0:T(8,128)(2,1)S(1)}, bf16[208,768]{1,0:T(8,128)(2,1)S(1)}, u32[]{:S(2)}, u32[]{:S(2)}) collective-permute-start(bf16[208,768]{1,0:T(8,128)(2,1)S(1)} %pad_maximum_fusion.10), channel_id=1, source_target_pairs={{0,8},{4,12},{8,0},{12,4},{1,9},{5,13},{9,1},{13,5},{2,10},{6,14},... | collective-permute-start | bytes 958472 | tf_op jit(solution)/shard_map/ppermute | solution.py:441
  278.1 29.5 %collective-permute-start.45 = (bf16[768,384]{1,0:T(8,128)(2,1)S(1)}, bf16[768,384]{1,0:T(8,128)(2,1)S(1)}, u32[]{:S(2)}, u32[]{:S(2)}) collective-permute-start(bf16[768,384]{1,0:T(8,128)(2,1)S(1)} %pad_maximum_fusion.5.refs_0_), channel_id=1, source_target_pairs={{0,1},{1,0},{2,3},{3,2},{4,5},{5,4},{6,7},{7,6},{8,9},{9,8},{10,11... | collective-permute-start | bytes 1769480 | tf_op jit(solution)/shard_map/ppermute | solution.py:441
  278.2 15.7 %collective-permute-start.44 = (bf16[768,384]{1,0:T(8,128)(2,1)S(1)}, bf16[768,384]{1,0:T(8,128)(2,1)S(1)}, u32[]{:S(2)}, u32[]{:S(2)}) collective-permute-start(bf16[768,384]{1,0:T(8,128)(2,1)S(1)} %pad_maximum_fusion.5.refs_0_), channel_id=1, source_target_pairs={{0,2},{1,3},{2,0},{3,1},{4,6},{5,7},{6,4},{7,5},{8,10},{9,11},{10,... | collective-permute-start | bytes 1769480 | tf_op jit(solution)/shard_map/ppermute | solution.py:441
  279.9 28.5 %collective-permute-start.49 = (bf16[768,384]{1,0:T(8,128)(2,1)S(1)}, bf16[768,384]{1,0:T(8,128)(2,1)S(1)}, u32[]{:S(2)}, u32[]{:S(2)}) collective-permute-start(bf16[768,384]{1,0:T(8,128)(2,1)S(1)} %pad_maximum_fusion.6.refs_4_), channel_id=1, source_target_pairs={{0,1},{1,0},{2,3},{3,2},{4,5},{5,4},{6,7},{7,6},{8,9},{9,8},{10,11... | collective-permute-start | bytes 1769480 | tf_op jit(solution)/shard_map/ppermute | solution.py:441
  285.6 16.2 %collective-permute-start.48 = (bf16[768,384]{1,0:T(8,128)(2,1)S(1)}, bf16[768,384]{1,0:T(8,128)(2,1)S(1)}, u32[]{:S(2)}, u32[]{:S(2)}) collective-permute-start(bf16[768,384]{1,0:T(8,128)(2,1)S(1)} %pad_maximum_fusion.6.refs_4_), channel_id=1, source_target_pairs={{0,16},{16,0},{1,17},{17,1},{2,18},{18,2},{3,19},{19,3},{4,20},{20... | collective-permute-start | bytes 1769480 | tf_op jit(solution)/shard_map/ppermute | solution.py:441
  286.1 15.8 %collective-permute-start.55 = (bf16[384,384]{1,0:T(8,128)(2,1)S(1)}, bf16[384,384]{1,0:T(8,128)(2,1)S(1)}, u32[]{:S(2)}, u32[]{:S(2)}) collective-permute-start(bf16[384,384]{1,0:T(8,128)(2,1)S(1)} %get-tuple-element.182), channel_id=1, source_target_pairs={{0,4},{4,0},{8,12},{12,8},{1,5},{5,1},{9,13},{13,9},{2,6},{6,2},{1... | collective-permute-start | bytes 884744 | tf_op jit(solution)/shard_map/ppermute | solution.py:441
  307.2 14.4 %collective-permute-start.56 = (bf16[768,384]{1,0:T(8,128)(2,1)S(1)}, bf16[768,384]{1,0:T(8,128)(2,1)S(1)}, u32[]{:S(2)}, u32[]{:S(2)}) collective-permute-start(bf16[768,384]{1,0:T(8,128)(2,1)S(1)} %pad_maximum_fusion.7), channel_id=1, source_target_pairs={{0,16},{16,0},{1,17},{17,1},{2,18},{18,2},{3,19},{19,3},{4,20},{20... | collective-permute-start | bytes 1769480 | tf_op jit(solution)/shard_map/ppermute | solution.py:441
  307.7 14.2 %collective-permute-start.58 = (bf16[768,384]{1,0:T(8,128)(2,1)S(1)}, bf16[768,384]{1,0:T(8,128)(2,1)S(1)}, u32[]{:S(2)}, u32[]{:S(2)}) collective-permute-start(bf16[768,384]{1,0:T(8,128)(2,1)S(1)} %pad_maximum_fusion.8), channel_id=1, source_target_pairs={{0,4},{4,0},{8,12},{12,8},{1,5},{5,1},{9,13},{13,9},{2,6},{6,2},{1... | collective-permute-start | bytes 1769480 | tf_op jit(solution)/shard_map/ppermute | solution.py:441
  (91 other events, 799.6 us)
where the time goes:
time: 326 us; the launch traced here: 325 us
  waiting for transfers between devices  157 us (48%)
  starting transfers between devices  52.2 us (16%)
  Pallas kernels  48.6 us (15%)
  local copies, waits for them, and re-layouts  19.4 us (6%)
  blocking collectives  16.7 us (5%)
  other arithmetic  15.1 us (5%)
  matrix products  13.3 us (4%)
  between operations  3.3 us (1%)
    ppermute x59, waiting for transfers between devices, hop(): lax.ppermute(value, axis, [(i, i ^ distance) for i in range(lax.axis_size...  157 us
    ppermute x59, starting transfers between devices, hop(): lax.ppermute(value, axis, [(i, i ^ distance) for i in range(lax.axis_size...  52.2 us
    pallas_call x1, Pallas kernels, key_side(): on_chip(kernel, jax.ShapeDtypeStruct((rows, 2 * wide), BF16), [acc, acc])  9.78 us
    unnamed x117, local copies, waits for them, and re-layouts  9.49 us
    pallas_call x1, Pallas kernels, query_side(): on_chip(kernel, jax.ShapeDtypeStruct((rows, wide), BF16), [pltpu.VMEM((ro...  8.8 us
    all_gather x1, blocking collectives, per_device(): lax.all_gather(hidden1.astype(BF16), 'weight', axis=0, tiled=True)  8.62 us
    all_gather x1, blocking collectives, per_device(): lax.all_gather(grad_resid2.astype(BF16), 'weight', axis=0, tiled=True)  8.09 us
    pallas_call x1, Pallas kernels, assemble(): pl.pallas_call(kernel, out_shape=(jax.ShapeDtypeStruct((width, 3 * width)...  6.65 us
  transfers between devices with their start and end apart: 59, of which 26 were waited for; matrix products, arithmetic and copies ran while one was open for 6% of the time, Pallas kernels for 8%

commit v1 on v0

--- a/solution.py
+++ b/solution.py
@@ -499,6 +499,13 @@
     return blocks
 
 
+def send_head(parts):
+    got = [parts[0]]
+    for at in range(1, len(parts)):
+        got.append(hop(parts[at], "head", at))
+    return got
+
+
 def gather_head(value):
     blocks = {0: value}
     for place in bits_of("head")[::-1]:
@@ -584,7 +591,7 @@
     ).astype(BF16)
     attended, logs, *parts = attend(query, keyvals, heads, head_devs)
     queries = gather_blocks(after(query, attended))
-    returned = [parts[0]] + [hop(parts[at], "head", at) for at in range(1, head_devs)]
+    returned = send_head(parts)
     returned = jnp.concatenate(returned, axis=1)
     resid1 = flat.astype(F32) + jnp.dot(returned, out_rows, preferred_element_type=F32) + out_bias
     hidden1, normed1, rstd1 = norm_forward(resid1, norm1_gain, norm1_bias)
@@ -635,7 +642,7 @@
     ffn_places = bits_of("blk")[1:] + bits_of("head")
     layer_out = from_sequence(after(final.astype(BF16), grad_half), BF16)
     backs = project_back(grad_half, out_rows, head_devs)
-    backs = [backs[0]] + [hop(backs[at], "head", at) for at in range(1, head_devs)]
+    backs = send_head(backs)
     back = with_stats(backs, attended, logs, heads)
     back_blocks = gather_blocks(back)
     grad_late = after(grad_half, back)

time: 326 us -> 326 us (level)
  no operation moved by 1% of the time
where the time goes in v1:
time: 326 us; the launch traced here: 325 us
  waiting for transfers between devices  157 us (48%)
  starting transfers between devices  52.2 us (16%)
  Pallas kernels  48.6 us (15%)
  local copies, waits for them, and re-layouts  19.4 us (6%)
  blocking collectives  16.7 us (5%)
  other arithmetic  15.1 us (5%)
  matrix products  13.3 us (4%)
  between operations  3.3 us (1%)
    ppermute x59, waiting for transfers between devices, hop(): lax.ppermute(value, axis, [(i, i ^ distance) for i in range(lax.axis_size...  157 us
    ppermute x59, starting transfers between devices, hop(): lax.ppermute(value, axis, [(i, i ^ distance) for i in range(lax.axis_size...  52.2 us
    pallas_call x1, Pallas kernels, key_side(): on_chip(kernel, jax.ShapeDtypeStruct((rows, 2 * wide), BF16), [acc, acc])  9.78 us
    unnamed x117, local copies, waits for them, and re-layouts  9.49 us
    pallas_call x1, Pallas kernels, query_side(): on_chip(kernel, jax.ShapeDtypeStruct((rows, wide), BF16), [pltpu.VMEM((ro...  8.8 us
    all_gather x1, blocking collectives, per_device(): lax.all_gather(hidden1.astype(BF16), 'weight', axis=0, tiled=True)  8.62 us
    all_gather x1, blocking collectives, per_device(): lax.all_gather(grad_resid2.astype(BF16), 'weight', axis=0, tiled=True)  8.09 us
    pallas_call x1, Pallas kernels, assemble(): pl.pallas_call(kernel, out_shape=(jax.ShapeDtypeStruct((width, 3 * width)...  6.65 us
  transfers between devices with their start and end apart: 59, of which 26 were waited for; matrix products, arithmetic and copies ran while one was open for 6% of the time, Pallas kernels for 8%

profile of v1, /device:TPU:0, one launch (start us, length us, event | category | flops | bytes accessed | tf_op | source)
XLA Modules:
  0.0 325.2 jit_solution(18404190784059524075)
XLA Ops:
  12.7 4.8 %prepare.1 = (bf16[768,256]{1,0:T(8,128)(2,1)}, bf16[768,512]{1,0:T(8,128)(2,1)}, f32[1,768]{1,0:T(1,128)}, bf16[1024,768]{1,0:T(8,128)(2,1)}) custom-call(s32[1]{0:T(128)} %bitcast.2.at_ref, bf16[768,2304]{1,0:T(8,128)(2,1)} %qkv_ref, bf16[768,768]{1,0:T(8,128)(2,1)} %out_ref.1, f32[1,768]{1,0:T(1,128)} %reshape.190.qb_ref, f32[1,768]{1,0:T(1,128)} %reshape.191.vb_ref), custom_call_target="tpu_custom_call" | custom-call | tf_op jit(solution)/shard_map/prepare/pallas_call | solution.py:142
  31.4 4.4 %collective-permute-done.7.refs_6_.refs_5_ = bf16[256,512]{1,0:T(8,128)(2,1)S(1)} collective-permute-done((bf16[256,512]{1,0:T(8,128)(2,1)S(1)}, bf16[256,512]{1,0:T(8,128)(2,1)S(1)}, u32[]{:S(2)}, u32[]{:S(2)}) %collective-permute-start.7) | collective-permute-done | bytes 262176 | tf_op jit(solution)/shard_map/ppermute | solution.py:441
  39.5 6.3 %shard_map.271 = (bf16[512,256]{1,0:T(8,128)(2,1)}, bf16[512,256]{1,0:T(8,128)(2,1)}, bf16[128,256]{1,0:T(8,128)(2,1)}, bf16[128,256]{1,0:T(8,128)(2,1)}, bf16[1...) custom-call(bf16[512,256]{1,0:T(8,128)(2,1)} %fusion.9.refs_0_.query_ref.refs_2_, bf16[256,512]{1,0:T(8,128)(2,1)} %copy-done.5, ...), custom_call_target="tpu_custom_call" | custom-call | tf_op jit(solution)/shard_map/pallas_call | solution.py:196
  52.2 4.0 %collective-permute-done.12 = bf16[128,256]{1,0:T(8,128)(2,1)S(1)} collective-permute-done((bf16[128,256]{1,0:T(8,128)(2,1)}, bf16[128,256]{1,0:T(8,128)(2,1)S(1)}, u32[]{:S(2)}, u32[]{:S(2)}) %collective-permute-start.12) | collective-permute-done | bytes 65568 | tf_op jit(solution)/shard_map/ppermute | solution.py:441
  58.0 8.6 %all_gather.6 = bf16[512,768]{1,0:T(8,128)(2,1)S(1)} all-gather(bf16[128,768]{1,0:T(8,128)(2,1)S(1)} %fusion.33), channel_id=1, replica_groups=mesh['blk'=2,'head'=4,'weight'=4] {'weight'}, dimensions={0}, use_global_device_ids=true | all-gather | bytes 983040 | tf_op jit(solution)/shard_map/all_gather | solution.py:598
  77.1 5.8 %collective-permute-done.14 = bf16[1,128,768]{2,1,0:T(8,128)(2,1)S(1)} collective-permute-done((bf16[1,128,768]{2,1,0:T(8,128)(2,1)S(1)}, bf16[1,128,768]{2,1,0:T(8,128)(2,1)S(1)}, u32[]{:S(2)}, u32[]{:S(2)}) %collective-permute-start.14) | collective-permute-done | bytes 196640 | tf_op jit(solution)/shard_map/ppermute | solution.py:441
  84.0 8.1 %all_gather.7 = bf16[512,768]{1,0:T(8,128)(2,1)S(1)} all-gather(bf16[128,768]{1,0:T(8,128)(2,1)S(1)} %convert_element_type.192), channel_id=1, replica_groups=mesh['blk'=2,'head'=4,'weight'=4] {'weight'}, dimensions={0}, use_global_device_ids=true | all-gather | bytes 983040 | tf_op jit(solution)/shard_map/all_gather | solution.py:612
  100.3 5.7 %collective-permute-done.17 = bf16[1,128,768]{2,1,0:T(8,128)(2,1)S(1)} collective-permute-done((bf16[1,128,768]{2,1,0:T(8,128)(2,1)S(1)}, bf16[1,128,768]{2,1,0:T(8,128)(2,1)S(1)}, u32[]{:S(2)}, u32[]{:S(2)}) %collective-permute-start.17) | collective-permute-done | bytes 196640 | tf_op jit(solution)/shard_map/ppermute | solution.py:441
  115.6 4.2 %collective-permute-done.20.refs_2_ = bf16[128,256]{1,0:T(8,128)(2,1)S(1)} collective-permute-done((bf16[128,256]{1,0:T(8,128)(2,1)}, bf16[128,256]{1,0:T(8,128)(2,1)S(1)}, u32[]{:S(2)}, u32[]{:S(2)}) %collective-permute-start.20) | collective-permute-done | bytes 65568 | tf_op jit(solution)/shard_map/ppermute | solution.py:441
  128.0 5.2 %collective-permute-done.30 = bf16[128,768]{1,0:T(8,128)(2,1)S(1)} collective-permute-done((bf16[128,768]{1,0:T(8,128)(2,1)S(1)}, bf16[128,768]{1,0:T(8,128)(2,1)S(1)}, u32[]{:S(2)}, u32[]{:S(2)}) %collective-permute-start.30) | collective-permute-done | bytes 196640 | tf_op jit(solution)/shard_map/ppermute | solution.py:441
  133.2 9.3 %collective-permute-done.29 = bf16[128,768]{1,0:T(8,128)(2,1)S(1)} collective-permute-done((bf16[128,768]{1,0:T(8,128)(2,1)S(1)}, bf16[128,768]{1,0:T(8,128)(2,1)S(1)}, u32[]{:S(2)}, u32[]{:S(2)}) %collective-permute-start.29) | collective-permute-done | bytes 196640 | tf_op jit(solution)/shard_map/ppermute | solution.py:441
  143.3 8.8 %shard_map.274.dq_ref = bf16[512,256]{1,0:T(8,128)(2,1)} custom-call(bf16[512,256]{1,0:T(8,128)(2,1)} %fusion.9.refs_0_.query_ref.refs_2_, bf16[512,256]{1,0:T(8,128)(2,1)} %shard_map.273.back_ref.refs_6_, bf16[256,512]{1,0:T(8,128)(2,1)} %copy-done.5, bf16[256,512]{1,0:T(8,128)(2,1)} %copy-done.11, bf16[256,512]{1,0:T(8,128)(2,1)} %copy-done.13, ...), custom_call_target="tpu_custom_call" | custom-call | tf_op jit(solution)/shard_map/pallas_call | solution.py:267
  154.6 9.8 %shard_map.275.dkv_ref = bf16[512,512]{1,0:T(8,128)(2,1)} custom-call(bf16[256,512]{1,0:T(8,128)(2,1)} %copy-done.5, bf16[256,512]{1,0:T(8,128)(2,1)} %copy-done.6, bf16[512,256]{1,0:T(8,128)(2,1)} %fusion.9.refs_0_.query_ref.refs_2_, bf16[512,256]{1,0:T(8,128)(2,1)} %copy-done.27, bf16[512,256]{1,0:T(8,128)(2,1)} %copy-done.29, ...), custom_call_target="tpu_custom_call" | custom-call | tf_op jit(solution)/shard_map/pallas_call | solution.py:308
  180.1 24.1 %collective-permute-done.51 = bf16[784,768]{1,0:T(8,128)(2,1)S(1)} collective-permute-done((bf16[784,768]{1,0:T(8,128)(2,1)S(1)}, bf16[784,768]{1,0:T(8,128)(2,1)S(1)}, u32[]{:S(2)}, u32[]{:S(2)}) %collective-permute-start.51) | collective-permute-done | bytes 1204256 | tf_op jit(solution)/shard_map/ppermute | solution.py:441
  214.6 5.3 %collective-permute-done.37 = bf16[112,768]{1,0:T(8,128)(2,1)S(1)} collective-permute-done((bf16[112,768]{1,0:T(8,128)(2,1)S(1)}, bf16[112,768]{1,0:T(8,128)(2,1)S(1)}, u32[]{:S(2)}, u32[]{:S(2)}) %collective-permute-start.37) | collective-permute-done | bytes 172064 | tf_op jit(solution)/shard_map/ppermute | solution.py:441
  220.8 14.4 %collective-permute-done.36 = bf16[112,768]{1,0:T(8,128)(2,1)S(1)} collective-permute-done((bf16[112,768]{1,0:T(8,128)(2,1)S(1)}, bf16[112,768]{1,0:T(8,128)(2,1)S(1)}, u32[]{:S(2)}, u32[]{:S(2)}) %collective-permute-start.36) | collective-permute-done | bytes 172064 | tf_op jit(solution)/shard_map/ppermute | solution.py:441
  244.4 25.4 %collective-permute-done.53 = bf16[208,768]{1,0:T(8,128)(2,1)S(1)} collective-permute-done((bf16[208,768]{1,0:T(8,128)(2,1)S(1)}, bf16[208,768]{1,0:T(8,128)(2,1)S(1)}, u32[]{:S(2)}, u32[]{:S(2)}) %collective-permute-start.53) | collective-permute-done | bytes 319520 | tf_op jit(solution)/shard_map/ppermute | solution.py:441
  272.3 5.7 %collective-permute-done.43 = bf16[384,384]{1,0:T(8,128)(2,1)S(1)} collective-permute-done((bf16[384,384]{1,0:T(8,128)(2,1)S(1)}, bf16[384,384]{1,0:T(8,128)(2,1)S(1)}, u32[]{:S(2)}, u32[]{:S(2)}) %collective-permute-start.43) | collective-permute-done | bytes 294944 | tf_op jit(solution)/shard_map/ppermute | solution.py:441
  280.2 5.5 %collective-permute-done.54 = bf16[192,768]{1,0:T(8,128)(2,1)S(1)} collective-permute-done((bf16[192,768]{1,0:T(8,128)(2,1)S(1)}, bf16[192,768]{1,0:T(8,128)(2,1)S(1)}, u32[]{:S(2)}, u32[]{:S(2)}) %collective-permute-start.54) | collective-permute-done | bytes 294944 | tf_op jit(solution)/shard_map/ppermute | solution.py:441
  287.3 6.7 %collective-permute-done.44.refs_1_ = bf16[768,384]{1,0:T(8,128)(2,1)S(1)} collective-permute-done((bf16[768,384]{1,0:T(8,128)(2,1)S(1)}, bf16[768,384]{1,0:T(8,128)(2,1)S(1)}, u32[]{:S(2)}, u32[]{:S(2)}) %collective-permute-start.44) | collective-permute-done | bytes 589856 | tf_op jit(solution)/shard_map/ppermute | solution.py:441
  295.7 6.1 %collective-permute-done.48.refs_5_ = bf16[768,384]{1,0:T(8,128)(2,1)S(1)} collective-permute-done((bf16[768,384]{1,0:T(8,128)(2,1)S(1)}, bf16[768,384]{1,0:T(8,128)(2,1)S(1)}, u32[]{:S(2)}, u32[]{:S(2)}) %collective-permute-start.48) | collective-permute-done | bytes 589856 | tf_op jit(solution)/shard_map/ppermute | solution.py:441
  302.5 4.7 %collective-permute-done.57 = bf16[384,384]{1,0:T(8,128)(2,1)S(1)} collective-permute-done((bf16[384,384]{1,0:T(8,128)(2,1)S(1)}, bf16[384,384]{1,0:T(8,128)(2,1)S(1)}, u32[]{:S(2)}, u32[]{:S(2)}) %collective-permute-start.57) | collective-permute-done | bytes 294944 | tf_op jit(solution)/shard_map/ppermute | solution.py:441
  310.3 6.6 %assemble.1 = (f32[768,2304]{1,0:T(8,128)}, f32[768,768]{1,0:T(8,128)}) custom-call(s32[4]{0:T(128)} %pad_add_fusion.1.at_ref, bf16[768,384]{1,0:T(8,128)(2,1)} %copy-done.3, bf16[768,384]{1,0:T(8,128)(2,1)} %copy-done.20, bf16[768,384]{1,0:T(8,128)(2,1)} %copy-done.19, bf16[768,384]{1,0:T(8,128)(2,1)} %copy-done.23, bf16[768,384]{1,0:T(8,128)(2,1)} %copy-done.4, ...), custom_call_target="tpu_custom_call" | custom-call | tf_op jit(solution)/shard_map/assemble/pallas_call | solution.py:413
  316.9 4.7 %collective-permute-done.56 = bf16[768,384]{1,0:T(8,128)(2,1)S(1)} collective-permute-done((bf16[768,384]{1,0:T(8,128)(2,1)S(1)}, bf16[768,384]{1,0:T(8,128)(2,1)S(1)}, u32[]{:S(2)}, u32[]{:S(2)}) %collective-permute-start.56) | collective-permute-done | bytes 589856 | tf_op jit(solution)/shard_map/ppermute | solution.py:441
  (361 shorter events, 127.7 us)
Async XLA Ops:
  122.8 19.7 %collective-permute-start.25 = (bf16[512,256]{1,0:T(8,128)(2,1)}, bf16[512,256]{1,0:T(8,128)(2,1)S(1)}, u32[]{:S(2)}, u32[]{:S(2)}) collective-permute-start(bf16[512,256]{1,0:T(8,128)(2,1)} %shard_map.273.back_ref.refs_6_), channel_id=1, source_target_pairs={{0,2},{1,3},{2,0},{3,1},{4,6},{5,7},{6,4},{7,5},{8,10},{9,11},{10,... | collective-permute-start | bytes 786440 | tf_op jit(solution)/shard_map/ppermute | solution.py:441
  125.9 16.6 %collective-permute-start.29 = (bf16[128,768]{1,0:T(8,128)(2,1)S(1)}, bf16[128,768]{1,0:T(8,128)(2,1)S(1)}, u32[]{:S(2)}, u32[]{:S(2)}) collective-permute-start(bf16[128,768]{1,0:T(8,128)(2,1)S(1)} %copy-done.8), channel_id=1, source_target_pairs={{0,8},{4,12},{8,0},{12,4},{1,9},{5,13},{9,1},{13,5},{2,10},{6,14},... | collective-permute-start | bytes 589832 | tf_op jit(solution)/shard_map/ppermute | solution.py:441
  126.3 25.8 %collective-permute-start.28 = (bf16[128,768]{1,0:T(8,128)(2,1)S(1)}, bf16[128,768]{1,0:T(8,128)(2,1)}, u32[]{:S(2)}, u32[]{:S(2)}) collective-permute-start(bf16[128,768]{1,0:T(8,128)(2,1)S(1)} %copy-done.8), channel_id=1, source_target_pairs={{0,4},{4,0},{8,12},{12,8},{1,5},{5,1},{9,13},{13,9},{2,6},{6,2},{1... | collective-permute-start | bytes 589832 | tf_op jit(solution)/shard_map/ppermute | solution.py:441
  128.0 26.0 %collective-permute-start.23 = (bf16[512,256]{1,0:T(8,128)(2,1)S(1)}, bf16[512,256]{1,0:T(8,128)(2,1)S(1)}, u32[]{:S(2)}, u32[]{:S(2)}) collective-permute-start(bf16[512,256]{1,0:T(8,128)(2,1)S(1)} %copy-done.7), channel_id=1, source_target_pairs={{0,1},{1,0},{2,3},{3,2},{4,5},{5,4},{6,7},{7,6},{8,9},{9,8},{10,11... | collective-permute-start | bytes 786440 | tf_op jit(solution)/shard_map/ppermute | solution.py:441
  133.2 20.8 %collective-permute-start.24 = (bf16[512,256]{1,0:T(8,128)(2,1)S(1)}, bf16[512,256]{1,0:T(8,128)(2,1)}, u32[]{:S(2)}, u32[]{:S(2)}) collective-permute-start(bf16[512,256]{1,0:T(8,128)(2,1)S(1)} %collective-permute-done.22.refs_3_), channel_id=1, source_target_pairs={{0,1},{1,0},{2,3},{3,2},{4,5},{5,4},{6,7},{7,6},{8,9},{9,8},{10,11... | collective-permute-start | bytes 786440 | tf_op jit(solution)/shard_map/ppermute | solution.py:441
  172.6 47.2 %collective-permute-start.18 = (bf16[64,768]{1,0:T(8,128)(2,1)S(1)}, bf16[64,768]{1,0:T(8,128)(2,1)S(1)}, u32[]{:S(2)}, u32[]{:S(2)}) collective-permute-start(bf16[64,768]{1,0:T(8,128)(2,1)S(1)} %slice.223), channel_id=1, source_target_pairs={{0,16},{16,0},{1,17},{17,1},{2,18},{18,2},{3,19},{19,3},{4,20},{20... | collective-permute-start | bytes 294920 | tf_op jit(solution)/shard_map/ppermute | solution.py:441
  173.2 31.0 %collective-permute-start.51 = (bf16[784,768]{1,0:T(8,128)(2,1)S(1)}, bf16[784,768]{1,0:T(8,128)(2,1)S(1)}, u32[]{:S(2)}, u32[]{:S(2)}) collective-permute-start(bf16[784,768]{1,0:T(8,128)(2,1)S(1)} %pad_maximum_fusion), channel_id=1, source_target_pairs={{0,16},{16,0},{1,17},{17,1},{2,18},{18,2},{3,19},{19,3},{4,20},{20... | collective-permute-start | bytes 3612680 | tf_op jit(solution)/shard_map/ppermute | solution.py:441
  178.3 26.4 %collective-permute-start.32 = (bf16[208,384]{1,0:T(8,128)(2,1)S(1)}, bf16[208,384]{1,0:T(8,128)(2,1)S(1)}, u32[]{:S(2)}, u32[]{:S(2)}) collective-permute-start(bf16[208,384]{1,0:T(8,128)(2,1)S(1)} %pad_maximum_fusion.15), channel_id=1, source_target_pairs={{0,2},{1,3},{2,0},{3,1},{4,6},{5,7},{6,4},{7,5},{8,10},{9,11},{10,... | collective-permute-start | bytes 479240 | tf_op jit(solution)/shard_map/ppermute | solution.py:441
  179.6 27.1 %collective-permute-start.33 = (bf16[208,384]{1,0:T(8,128)(2,1)S(1)}, bf16[208,384]{1,0:T(8,128)(2,1)S(1)}, u32[]{:S(2)}, u32[]{:S(2)}) collective-permute-start(bf16[208,384]{1,0:T(8,128)(2,1)S(1)} %pad_maximum_fusion.16), channel_id=1, source_target_pairs={{0,16},{16,0},{1,17},{17,1},{2,18},{18,2},{3,19},{19,3},{4,20},{20... | collective-permute-start | bytes 479240 | tf_op jit(solution)/shard_map/ppermute | solution.py:441
  212.3 31.0 %collective-permute-start.52 = (bf16[400,768]{1,0:T(8,128)(2,1)S(1)}, bf16[400,768]{1,0:T(8,128)(2,1)S(1)}, u32[]{:S(2)}, u32[]{:S(2)}) collective-permute-start(bf16[400,768]{1,0:T(8,128)(2,1)S(1)} %pad_maximum_fusion.3), channel_id=1, source_target_pairs={{0,4},{4,0},{8,12},{12,8},{1,5},{5,1},{9,13},{13,9},{2,6},{6,2},{1... | collective-permute-start | bytes 1843208 | tf_op jit(solution)/shard_map/ppermute | solution.py:441
  214.5 20.7 %collective-permute-start.36 = (bf16[112,768]{1,0:T(8,128)(2,1)S(1)}, bf16[112,768]{1,0:T(8,128)(2,1)S(1)}, u32[]{:S(2)}, u32[]{:S(2)}) collective-permute-start(bf16[112,768]{1,0:T(8,128)(2,1)S(1)} %maximum_maximum_fusion), channel_id=1, source_target_pairs={{0,4},{4,0},{8,12},{12,8},{1,5},{5,1},{9,13},{13,9},{2,6},{6,2},{1... | collective-permute-start | bytes 516104 | tf_op jit(solution)/shard_map/ppermute | solution.py:441
  219.8 17.3 %collective-permute-start.38 = (bf16[112,768]{1,0:T(8,128)(2,1)S(1)}, bf16[112,768]{1,0:T(8,128)(2,1)S(1)}, u32[]{:S(2)}, u32[]{:S(2)}) collective-permute-start(bf16[112,768]{1,0:T(8,128)(2,1)S(1)} %collective-permute-done.37), channel_id=1, source_target_pairs={{0,4},{4,0},{8,12},{12,8},{1,5},{5,1},{9,13},{13,9},{2,6},{6,2},{1... | collective-permute-start | bytes 516104 | tf_op jit(solution)/shard_map/ppermute | solution.py:441
  237.2 34.6 %collective-permute-start.39 = (bf16[128,768]{1,0:T(8,128)(2,1)S(1)}, bf16[128,768]{1,0:T(8,128)(2,1)S(1)}, u32[]{:S(2)}, u32[]{:S(2)}) collective-permute-start(bf16[128,768]{1,0:T(8,128)(2,1)S(1)} %copy-done.52), channel_id=1, source_target_pairs={{0,4},{4,0},{8,12},{12,8},{1,5},{5,1},{9,13},{13,9},{2,6},{6,2},{1... | collective-permute-start | bytes 589832 | tf_op jit(solution)/shard_map/ppermute | solution.py:441
  237.3 34.6 %collective-permute-start.40 = (bf16[128,768]{1,0:T(8,128)(2,1)S(1)}, bf16[128,768]{1,0:T(8,128)(2,1)S(1)}, u32[]{:S(2)}, u32[]{:S(2)}) collective-permute-start(bf16[128,768]{1,0:T(8,128)(2,1)S(1)} %copy-done.51), channel_id=1, source_target_pairs={{0,8},{4,12},{8,0},{12,4},{1,9},{5,13},{9,1},{13,5},{2,10},{6,14},... | collective-permute-start | bytes 589832 | tf_op jit(solution)/shard_map/ppermute | solution.py:441
  240.0 31.8 %collective-permute-start.41 = (bf16[128,768]{1,0:T(8,128)(2,1)S(1)}, bf16[128,768]{1,0:T(8,128)(2,1)S(1)}, u32[]{:S(2)}, u32[]{:S(2)}) collective-permute-start(bf16[128,768]{1,0:T(8,128)(2,1)S(1)} %copy-done.50), channel_id=1, source_target_pairs={{0,12},{4,8},{8,4},{12,0},{1,13},{5,9},{9,5},{13,1},{2,14},{6,10},... | collective-permute-start | bytes 589832 | tf_op jit(solution)/shard_map/ppermute | solution.py:441
  241.7 38.1 %collective-permute-start.47 = (bf16[384,384]{1,0:T(8,128)(2,1)S(1)}, bf16[384,384]{1,0:T(8,128)(2,1)S(1)}, u32[]{:S(2)}, u32[]{:S(2)}) collective-permute-start(bf16[384,384]{1,0:T(8,128)(2,1)S(1)} %get-tuple-element.188), channel_id=1, source_target_pairs={{0,2},{1,3},{2,0},{3,1},{4,6},{5,7},{6,4},{7,5},{8,10},{9,11},{10,... | collective-permute-start | bytes 884744 | tf_op jit(solution)/shard_map/ppermute | solution.py:441
  243.6 26.2 %collective-permute-start.53 = (bf16[208,768]{1,0:T(8,128)(2,1)S(1)}, bf16[208,768]{1,0:T(8,128)(2,1)S(1)}, u32[]{:S(2)}, u32[]{:S(2)}) collective-permute-start(bf16[208,768]{1,0:T(8,128)(2,1)S(1)} %pad_maximum_fusion.10), channel_id=1, source_target_pairs={{0,8},{4,12},{8,0},{12,4},{1,9},{5,13},{9,1},{13,5},{2,10},{6,14},... | collective-permute-start | bytes 958472 | tf_op jit(solution)/shard_map/ppermute | solution.py:441
  278.1 29.5 %collective-permute-start.45 = (bf16[768,384]{1,0:T(8,128)(2,1)S(1)}, bf16[768,384]{1,0:T(8,128)(2,1)S(1)}, u32[]{:S(2)}, u32[]{:S(2)}) collective-permute-start(bf16[768,384]{1,0:T(8,128)(2,1)S(1)} %pad_maximum_fusion.5.refs_0_), channel_id=1, source_target_pairs={{0,1},{1,0},{2,3},{3,2},{4,5},{5,4},{6,7},{7,6},{8,9},{9,8},{10,11... | collective-permute-start | bytes 1769480 | tf_op jit(solution)/shard_map/ppermute | solution.py:441
  278.2 15.7 %collective-permute-start.44 = (bf16[768,384]{1,0:T(8,128)(2,1)S(1)}, bf16[768,384]{1,0:T(8,128)(2,1)S(1)}, u32[]{:S(2)}, u32[]{:S(2)}) collective-permute-start(bf16[768,384]{1,0:T(8,128)(2,1)S(1)} %pad_maximum_fusion.5.refs_0_), channel_id=1, source_target_pairs={{0,2},{1,3},{2,0},{3,1},{4,6},{5,7},{6,4},{7,5},{8,10},{9,11},{10,... | collective-permute-start | bytes 1769480 | tf_op jit(solution)/shard_map/ppermute | solution.py:441
  279.9 28.5 %collective-permute-start.49 = (bf16[768,384]{1,0:T(8,128)(2,1)S(1)}, bf16[768,384]{1,0:T(8,128)(2,1)S(1)}, u32[]{:S(2)}, u32[]{:S(2)}) collective-permute-start(bf16[768,384]{1,0:T(8,128)(2,1)S(1)} %pad_maximum_fusion.6.refs_4_), channel_id=1, source_target_pairs={{0,1},{1,0},{2,3},{3,2},{4,5},{5,4},{6,7},{7,6},{8,9},{9,8},{10,11... | collective-permute-start | bytes 1769480 | tf_op jit(solution)/shard_map/ppermute | solution.py:441
  285.6 16.2 %collective-permute-start.48 = (bf16[768,384]{1,0:T(8,128)(2,1)S(1)}, bf16[768,384]{1,0:T(8,128)(2,1)S(1)}, u32[]{:S(2)}, u32[]{:S(2)}) collective-permute-start(bf16[768,384]{1,0:T(8,128)(2,1)S(1)} %pad_maximum_fusion.6.refs_4_), channel_id=1, source_target_pairs={{0,16},{16,0},{1,17},{17,1},{2,18},{18,2},{3,19},{19,3},{4,20},{20... | collective-permute-start | bytes 1769480 | tf_op jit(solution)/shard_map/ppermute | solution.py:441
  286.1 15.8 %collective-permute-start.55 = (bf16[384,384]{1,0:T(8,128)(2,1)S(1)}, bf16[384,384]{1,0:T(8,128)(2,1)S(1)}, u32[]{:S(2)}, u32[]{:S(2)}) collective-permute-start(bf16[384,384]{1,0:T(8,128)(2,1)S(1)} %get-tuple-element.182), channel_id=1, source_target_pairs={{0,4},{4,0},{8,12},{12,8},{1,5},{5,1},{9,13},{13,9},{2,6},{6,2},{1... | collective-permute-start | bytes 884744 | tf_op jit(solution)/shard_map/ppermute | solution.py:441
  307.2 14.4 %collective-permute-start.56 = (bf16[768,384]{1,0:T(8,128)(2,1)S(1)}, bf16[768,384]{1,0:T(8,128)(2,1)S(1)}, u32[]{:S(2)}, u32[]{:S(2)}) collective-permute-start(bf16[768,384]{1,0:T(8,128)(2,1)S(1)} %pad_maximum_fusion.7), channel_id=1, source_target_pairs={{0,16},{16,0},{1,17},{17,1},{2,18},{18,2},{3,19},{19,3},{4,20},{20... | collective-permute-start | bytes 1769480 | tf_op jit(solution)/shard_map/ppermute | solution.py:441
  307.7 14.2 %collective-permute-start.58 = (bf16[768,384]{1,0:T(8,128)(2,1)S(1)}, bf16[768,384]{1,0:T(8,128)(2,1)S(1)}, u32[]{:S(2)}, u32[]{:S(2)}) collective-permute-start(bf16[768,384]{1,0:T(8,128)(2,1)S(1)} %pad_maximum_fusion.8), channel_id=1, source_target_pairs={{0,4},{4,0},{8,12},{12,8},{1,5},{5,1},{9,13},{13,9},{2,6},{6,2},{1... | collective-permute-start | bytes 1769480 | tf_op jit(solution)/shard_map/ppermute | solution.py:441
  (91 other events, 799.6 us)
